TPU v7x, 32 devices: a whole 2x2x4 slice. The times are simulated.
32 devices in a mesh: grp: 4 (over y, x), row: 8 (over z, core).
Axes of the slice: x: 2, y: 2, z: 4, core: 2. Of those that a mesh axis runs over, the one named last changes fastest.
Arguments:
- matrix_tiles: float32 [128, 32, 128, 128], P(('grp', 'row')), may hold values from -2 to 2, as said below
- column_index: int32 [128, 32], P(('grp', 'row')), may hold values from 0 to 127, as said below
- precond: float32 [128, 128, 128], P(('grp', 'row')), may hold values from -12 to 16, as said below
- right_side: float32 [128, 16, 128], P(('grp', 'row')), may hold values from -60 to 60
- lost_group: int32 [1], replicated, may hold values from 0 to 16383
Outputs:
- recovered: float32 [128, 16, 128], P(('grp', 'row'))
- true_residual: float32 [128, 16, 128], P(('grp', 'row'))
Inputs may be any that keep to these rules, and one draw needn't show every extreme that they name: `column_index`: entry 0 of block row i is i; entry 1 is i + 12, or i - 12 where i + 12 passes the end; every entry lies within 12 of its block row. `precond`: every block is symmetric positive definite. `matrix_tiles`: the diagonal tile of each block row is near the identity.
All inputs are finite; a program needn't handle non-finite values.
Results may differ from a plain program's by a relative error of at most 0.0003.
Values sent between devices are 32-bit elements; how exact they have to be, the bound alone decides.
No kernel may reach another device: no remote copies, remote signals or barrier semaphores. Data moves between devices by JAX's collectives and lax.ppermute only.
A program may use at most 64 MiB of HBM per device.

v0:
```python
import jax
import jax.numpy as jnp
from jax import lax
from jax.sharding import PartitionSpec as P

REACH = 3
OUTER = 2
INNER = 2
BAND = 12


def from_behind(value, axis, steps):
    count = lax.axis_size(axis)
    first, last = (max(0, -steps), min(count, count - steps))
    return lax.ppermute(value, axis, [(source, source + steps) for source in range(first, last)])


def inner_products(former, latter):
    return jnp.einsum("ica,ida->cd", former, latter, precision=lax.Precision.HIGHEST)


def scaled_by(vector, coeffs):
    return jnp.einsum("ica,cd->ida", vector, coeffs, precision=lax.Precision.HIGHEST)


def small_product(former, latter):
    return jnp.dot(former, latter, precision=lax.Precision.HIGHEST)


def solve_sym(matrix, target):
    factor = jnp.linalg.cholesky(0.5 * (matrix + matrix.T))
    middle = lax.linalg.triangular_solve(factor, target, left_side=True, lower=True)
    return lax.linalg.triangular_solve(factor, middle, left_side=True, lower=True, transpose_a=True)


def neighbour(vector, offset):
    return from_behind(vector, ("grp", "row"), offset)


def group_neighbour(vector, offset):
    return from_behind(vector, "row", offset)


def window_of(vector, shifter):
    pieces = [shifter(vector, offset) for offset in range(REACH, 0, -1)]
    pieces.append(vector)
    for offset in range(1, REACH + 1):
        pieces.append(shifter(vector, -offset))
    return jnp.concatenate(pieces, 0)


def tile_product(matrix_tiles, window, local_cols, kept_mask):
    picked = jnp.take(window, local_cols, axis=0)
    if kept_mask is not None:
        picked = picked * kept_mask[:, :, None, None]
    return jnp.einsum("ikab,ikcb->ica", matrix_tiles, picked, precision=lax.Precision.HIGHEST)


def per_device(matrix_tiles, column_index, precond, right_side, lost_group):
    blocks = right_side.shape[0]
    row_count = lax.axis_size("row")
    group_count = lax.axis_size("grp")
    group_blocks = blocks * row_count
    my_group = lax.axis_index("grp")
    my_start = lax.axis_index(("grp", "row")) * blocks
    local_cols = column_index - (my_start - BAND)
    other_mask = (column_index // group_blocks != my_group).astype(jnp.float32)
    own_mask = 1.0 - other_mask
    lost = lost_group[0] % group_count

    def full_product(vector):
        return tile_product(matrix_tiles, window_of(vector, neighbour), local_cols, None)

    solution = jnp.zeros_like(right_side)
    residual = right_side
    direction = right_side
    squares = lax.psum(inner_products(residual, residual), ("grp", "row"))
    for outer_step in range(OUTER):
        applied = full_product(direction)
        curvature, crossed, square = lax.psum(
            (
                inner_products(direction, applied),
                inner_products(applied, residual),
                inner_products(applied, applied),
            ),
            ("grp", "row"),
        )
        advance = solve_sym(curvature, squares)
        solution = solution + scaled_by(direction, advance)
        residual = residual - scaled_by(applied, advance)
        squares_next = (
            squares
            - small_product(crossed.T, advance)
            - small_product(advance.T, crossed)
            + small_product(advance.T, small_product(square, advance))
        )
        mixing = solve_sym(squares, squares_next)
        direction = residual + scaled_by(direction, mixing)
        squares = squares_next
    coupled = tile_product(matrix_tiles, window_of(solution, neighbour), local_cols, other_mask)
    inner_target = right_side - coupled

    def condition(vector):
        return jnp.einsum("iab,icb->ica", precond, vector, precision=lax.Precision.HIGHEST)

    estimate = jnp.zeros_like(inner_target)
    remainder = inner_target
    smoothed = condition(remainder)
    heading = smoothed
    weight = lax.psum(inner_products(remainder, smoothed), "row")
    for inner_step in range(INNER):
        applied = tile_product(
            matrix_tiles, window_of(heading, group_neighbour), local_cols, own_mask
        )
        bending = lax.psum(inner_products(heading, applied), "row")
        advance = solve_sym(bending, weight)
        estimate = estimate + scaled_by(heading, advance)
        remainder = remainder - scaled_by(applied, advance)
        if inner_step + 1 < INNER:
            smoothed = condition(remainder)
            weight_next = lax.psum(inner_products(remainder, smoothed), "row")
            heading = smoothed + scaled_by(heading, solve_sym(weight, weight_next))
            weight = weight_next
    recovered = jnp.where(my_group == lost, estimate, solution)
    true_residual = right_side - full_product(recovered)
    return (recovered, true_residual)


def solution(mesh):
    in_specs = (
        P(("grp", "row"), None, None, None),
        P(("grp", "row"), None),
        P(("grp", "row"), None, None),
        P(("grp", "row"), None, None),
        P(),
    )
    out_specs = (P(("grp", "row"), None, None), P(("grp", "row"), None, None))
    return jax.shard_map(
        per_device, mesh=mesh, in_specs=in_specs, out_specs=out_specs, check_vma=False
    )
```

profile of v0, /device:TPU:5, one launch (start us, length us, event | category | flops | bytes accessed | tf_op | source)
XLA Modules:
  0.0 370.1 jit_solution(12967061510973747642)
XLA Ops:
  0.6 6.8 %collective-permute-start.5 = (f32[4,16,128]{2,1,0:T(8,128)}, f32[4,16,128]{2,1,0:T(8,128)S(1)}, u32[]{:S(2)}, u32[]{:S(2)}) collective-permute-start(f32[4,16,128]{2,1,0:T(8,128)} %param.15), channel_id=1, source_target_pairs={{3,0},{4,1},{5,2},{6,3},{7,4},{8,5},{9,6},{10,7},{11,8},{12,9},{13... | collective-permute-start | bytes 98312 | tf_op jit(solution)/shard_map/ppermute | solution.py:15
  11.7 3.4 collective-permute-start.2
  19.8 4.3 %collective-permute-done = f32[4,16,128]{2,1,0:T(8,128)S(1)} collective-permute-done((f32[4,16,128]{2,1,0:T(8,128)}, f32[4,16,128]{2,1,0:T(8,128)S(1)}, u32[]{:S(2)}, u32[]{:S(2)}) %collective-permute-start) | collective-permute-done | bytes 32800 | tf_op jit(solution)/shard_map/ppermute | solution.py:15
  26.1 6.5 %collective-permute-done.1 = f32[4,16,128]{2,1,0:T(8,128)S(1)} collective-permute-done((f32[4,16,128]{2,1,0:T(8,128)}, f32[4,16,128]{2,1,0:T(8,128)S(1)}, u32[]{:S(2)}, u32[]{:S(2)}) %collective-permute-start.1) | collective-permute-done | bytes 32800 | tf_op jit(solution)/shard_map/ppermute | solution.py:15
  34.2 9.4 %convolution_bitcast_fusion.9 = f32[4,16,128]{2,1,0:T(8,128)S(1)} fusion(f32[4,32,128,128]{3,2,1,0:T(8,128)} %param.12, f32[4,32,16,128]{3,2,1,0:T(8,128)S(1)} %bitcast.254, pred[4,32]{1,0:T(4,128)(4,1)S(1)} %get-tuple-element.14), kind=kOutput, calls=%fused_computation.26 | convolution fusion | flops 402915328 | bytes 9470080 | tf_op jit(solution)/shard_map/ikab,ikcb->ica/dot_general | solution.py:56
  44.0 36.1 %all-reduce = (f32[16,16]{1,0:T(8,128)S(1)}, f32[16,16]{1,0:T(8,128)S(1)}, f32[16,16]{1,0:T(8,128)S(1)}, f32[16,16]{1,0:T(8,128)S(1)}) all-reduce(f32[16,16]{1,0:T(8,128)S(1)} %convolution_bitcast_fusion.21, f32[16,16]{1,0:T(8,128)S(1)} %bitcast.256, ...), channel_id=1, replica_groups=mesh['grp'=4,'row'=8] {'grp','row'}, use_global_device_ids=true, to_apply=%region_3.6 | all-reduce | flops 1024 | bytes 8192 | tf_op jit(solution)/shard_map/psum | solution.py:77
  90.4 6.3 %collective-permute-start.6 = (f32[4,16,128]{2,1,0:T(8,128)S(1)}, f32[4,16,128]{2,1,0:T(8,128)S(1)}, u32[]{:S(2)}, u32[]{:S(2)}) collective-permute-start(f32[4,16,128]{2,1,0:T(8,128)S(1)} %fusion.7), channel_id=1, source_target_pairs={{0,3},{1,4},{2,5},{3,6},{4,7},{5,8},{6,9},{7,10},{8,11},{9,12},{10... | collective-permute-start | bytes 98312 | tf_op jit(solution)/shard_map/ppermute | solution.py:15
  99.8 4.8 %collective-permute-start.10 = (f32[4,16,128]{2,1,0:T(8,128)S(1)}, f32[4,16,128]{2,1,0:T(8,128)S(1)}, u32[]{:S(2)}, u32[]{:S(2)}) collective-permute-start(f32[4,16,128]{2,1,0:T(8,128)S(1)} %fusion.7), channel_id=1, source_target_pairs={{2,0},{3,1},{4,2},{5,3},{6,4},{7,5},{8,6},{9,7},{10,8},{11,9},{12,... | collective-permute-start | bytes 98312 | tf_op jit(solution)/shard_map/ppermute | solution.py:15
  106.5 3.6 collective-permute-start.8
  112.7 5.8 %collective-permute-done.7 = f32[4,16,128]{2,1,0:T(8,128)S(1)} collective-permute-done((f32[4,16,128]{2,1,0:T(8,128)S(1)}, f32[4,16,128]{2,1,0:T(8,128)S(1)}, u32[]{:S(2)}, u32[]{:S(2)}) %collective-permute-start.7) | collective-permute-done | bytes 32800 | tf_op jit(solution)/shard_map/ppermute | solution.py:15
  119.3 9.4 %convolution_bitcast_fusion.6 = f32[4,16,128]{2,1,0:T(8,128)S(1)} fusion(f32[4,32,128,128]{3,2,1,0:T(8,128)} %param.12, f32[4,32,16,128]{3,2,1,0:T(8,128)S(1)} %bitcast.255, pred[4,32]{1,0:T(4,128)(4,1)S(1)} %get-tuple-element.14), kind=kOutput, calls=%fused_computation.21 | convolution fusion | flops 402915328 | bytes 9470080 | tf_op jit(solution)/shard_map/ikab,ikcb->ica/dot_general | solution.py:56
  128.8 36.1 %psum.67 = f32[16,16]{1,0:T(8,128)S(1)} all-reduce(f32[16,16]{1,0:T(8,128)S(1)} %convolution_bitcast_fusion.18), channel_id=1, replica_groups=mesh['grp'=4,'row'=8] {'grp','row'}, use_global_device_ids=true, to_apply=%region_6.11 | all-reduce | flops 256 | bytes 2048 | tf_op jit(solution)/shard_map/psum | solution.py:80
  169.7 6.0 %collective-permute-start.12 = (f32[4,16,128]{2,1,0:T(8,128)S(1)}, f32[4,16,128]{2,1,0:T(8,128)S(1)}, u32[]{:S(2)}, u32[]{:S(2)}) collective-permute-start(f32[4,16,128]{2,1,0:T(8,128)S(1)} %fusion.6), channel_id=1, source_target_pairs={{0,3},{1,4},{2,5},{3,6},{4,7},{5,8},{6,9},{7,10},{8,11},{9,12},{10... | collective-permute-start | bytes 98312 | tf_op jit(solution)/shard_map/ppermute | solution.py:15
  176.4 3.2 collective-permute-start.17
  179.6 4.4 %collective-permute-start.16 = (f32[4,16,128]{2,1,0:T(8,128)S(1)}, f32[4,16,128]{2,1,0:T(8,128)S(1)}, u32[]{:S(2)}, u32[]{:S(2)}) collective-permute-start(f32[4,16,128]{2,1,0:T(8,128)S(1)} %fusion.6), channel_id=1, source_target_pairs={{2,0},{3,1},{4,2},{5,3},{6,4},{7,5},{8,6},{9,7},{10,8},{11,9},{12,... | collective-permute-start | bytes 98312 | tf_op jit(solution)/shard_map/ppermute | solution.py:15
  186.0 3.6 collective-permute-start.14
  192.3 5.6 %collective-permute-done.13 = f32[4,16,128]{2,1,0:T(8,128)S(1)} collective-permute-done((f32[4,16,128]{2,1,0:T(8,128)S(1)}, f32[4,16,128]{2,1,0:T(8,128)S(1)}, u32[]{:S(2)}, u32[]{:S(2)}) %collective-permute-start.13) | collective-permute-done | bytes 32800 | tf_op jit(solution)/shard_map/ppermute | solution.py:15
  198.8 9.4 %fusion.5 = f32[4,16,128]{2,1,0:T(8,128)S(1)} fusion(f32[4,16,128]{2,1,0:T(8,128)S(1)} %copy-done.1, f32[4,32,128,128]{3,2,1,0:T(8,128)} %param.12, f32[4,32,16,128]{3,2,1,0:T(8,128)S(1)} %bitcast.250, f32[4,32]{1,0:T(4,128)S(1)} %get-tuple-element.13, pred[4,32]{1,0:T(4,128)(4,1)S(1)} %get-tuple-element.14), kind=kOutput, calls=%fused_computation.18 | convolution fusion | flops 403185664 | bytes 9503360 | tf_op jit(solution)/shard_map/ikab,ikcb->ica/dot_general | solution.py:56
  214.7 4.1 %collective-permute-start.20 = (f32[4,16,128]{2,1,0:T(8,128)S(1)}, f32[4,16,128]{2,1,0:T(8,128)S(1)}, u32[]{:S(2)}, u32[]{:S(2)}) collective-permute-start(f32[4,16,128]{2,1,0:T(8,128)S(1)} %fusion.85), channel_id=1, source_target_pairs={{0,1},{1,2},{2,3},{3,4},{4,5},{5,6},{6,7},{8,9},{9,10},{10,11},{11... | collective-permute-start | bytes 98312 | tf_op jit(solution)/shard_map/ppermute | solution.py:15
  218.8 4.0 %collective-permute-start.19 = (f32[4,16,128]{2,1,0:T(8,128)S(1)}, f32[4,16,128]{2,1,0:T(8,128)S(1)}, u32[]{:S(2)}, u32[]{:S(2)}) collective-permute-start(f32[4,16,128]{2,1,0:T(8,128)S(1)} %fusion.85), channel_id=1, source_target_pairs={{0,2},{1,3},{2,4},{3,5},{4,6},{5,7},{8,10},{9,11},{10,12},{11,13},... | collective-permute-start | bytes 98312 | tf_op jit(solution)/shard_map/ppermute | solution.py:15
  224.7 9.4 %convolution_bitcast_fusion.4 = f32[4,16,128]{2,1,0:T(8,128)S(1)} fusion(f32[4,32,128,128]{3,2,1,0:T(8,128)} %param.12, f32[4,32,16,128]{3,2,1,0:T(8,128)S(1)} %bitcast.251, f32[4,32]{1,0:T(4,128)S(1)} %get-tuple-element.12, pred[4,32]{1,0:T(4,128)(4,1)S(1)} %get-tuple-element.14), kind=kOutput, calls=%fused_computation.16 | convolution fusion | flops 403177472 | bytes 9470592 | tf_op jit(solution)/shard_map/ikab,ikcb->ica/dot_general | solution.py:56
  234.2 24.9 %all-reduce.1 = (f32[16,16]{1,0:T(8,128)S(1)}, f32[16,16]{1,0:T(8,128)S(1)}) all-reduce(f32[16,16]{1,0:T(8,128)S(1)} %convolution_bitcast_fusion.15, f32[16,16]{1,0:T(8,128)S(1)} %convolution_bitcast_fusion.16), channel_id=1, replica_groups=mesh['grp'=4,'row'=8] {'row'}, use_global_device_ids=true, to_apply=%region_8.13 | all-reduce | flops 512 | bytes 4096 | tf_op jit(solution)/shard_map/psum | solution.py:110
  268.8 17.3 %psum.70 = f32[16,16]{1,0:T(8,128)S(1)} all-reduce(f32[16,16]{1,0:T(8,128)S(1)} %convolution_bitcast_fusion.13), channel_id=1, replica_groups=mesh['grp'=4,'row'=8] {'row'}, use_global_device_ids=true, to_apply=%region_9.14 | all-reduce | flops 256 | bytes 2048 | tf_op jit(solution)/shard_map/psum | solution.py:121
  293.4 4.2 %collective-permute-start.26 = (f32[4,16,128]{2,1,0:T(8,128)S(1)}, f32[4,16,128]{2,1,0:T(8,128)S(1)}, u32[]{:S(2)}, u32[]{:S(2)}) collective-permute-start(f32[4,16,128]{2,1,0:T(8,128)S(1)} %fusion.3), channel_id=1, source_target_pairs={{0,1},{1,2},{2,3},{3,4},{4,5},{5,6},{6,7},{8,9},{9,10},{10,11},{11... | collective-permute-start | bytes 98312 | tf_op jit(solution)/shard_map/ppermute | solution.py:15
  297.5 4.2 %collective-permute-start.25 = (f32[4,16,128]{2,1,0:T(8,128)S(1)}, f32[4,16,128]{2,1,0:T(8,128)S(1)}, u32[]{:S(2)}, u32[]{:S(2)}) collective-permute-start(f32[4,16,128]{2,1,0:T(8,128)S(1)} %fusion.3), channel_id=1, source_target_pairs={{0,2},{1,3},{2,4},{3,5},{4,6},{5,7},{8,10},{9,11},{10,12},{11,13},... | collective-permute-start | bytes 98312 | tf_op jit(solution)/shard_map/ppermute | solution.py:15
  303.4 9.4 %convolution_bitcast_fusion.1 = f32[4,16,128]{2,1,0:T(8,128)S(1)} fusion(f32[4,32,128,128]{3,2,1,0:T(8,128)} %param.12, f32[4,32,16,128]{3,2,1,0:T(8,128)S(1)} %bitcast.252, f32[4,32]{1,0:T(4,128)S(1)} %get-tuple-element.12, pred[4,32]{1,0:T(4,128)(4,1)S(1)} %get-tuple-element.14), kind=kOutput, calls=%fused_computation.11 | convolution fusion | flops 403177472 | bytes 9470592 | tf_op jit(solution)/shard_map/ikab,ikcb->ica/dot_general | solution.py:56
  313.0 13.9 %psum.71 = f32[16,16]{1,0:T(8,128)S(1)} all-reduce(f32[16,16]{1,0:T(8,128)S(1)} %convolution_bitcast_fusion.11), channel_id=1, replica_groups=mesh['grp'=4,'row'=8] {'row'}, use_global_device_ids=true, to_apply=%region_10.15 | all-reduce | flops 256 | bytes 2048 | tf_op jit(solution)/shard_map/psum | solution.py:115
  333.6 7.2 %collective-permute-start.35 = (f32[4,16,128]{2,1,0:T(8,128)S(1)}, f32[4,16,128]{2,1,0:T(8,128)S(1)}, u32[]{:S(2)}, u32[]{:S(2)}) collective-permute-start(f32[4,16,128]{2,1,0:T(8,128)S(1)} %fusion.2), channel_id=1, source_target_pairs={{3,0},{4,1},{5,2},{6,3},{7,4},{8,5},{9,6},{10,7},{11,8},{12,9},{13... | collective-permute-start | bytes 98312 | tf_op jit(solution)/shard_map/ppermute | solution.py:15
  342.8 4.0 %collective-permute-start.33 = (f32[4,16,128]{2,1,0:T(8,128)S(1)}, f32[4,16,128]{2,1,0:T(8,128)S(1)}, u32[]{:S(2)}, u32[]{:S(2)}) collective-permute-start(f32[4,16,128]{2,1,0:T(8,128)S(1)} %fusion.2), channel_id=1, source_target_pairs={{1,0},{2,1},{3,2},{4,3},{5,4},{6,5},{7,6},{8,7},{9,8},{10,9},{11,1... | collective-permute-start | bytes 98312 | tf_op jit(solution)/shard_map/ppermute | solution.py:15
  346.8 3.5 collective-permute-start.32
  352.4 6.8 %collective-permute-done.31 = f32[4,16,128]{2,1,0:T(8,128)S(1)} collective-permute-done((f32[4,16,128]{2,1,0:T(8,128)S(1)}, f32[4,16,128]{2,1,0:T(8,128)S(1)}, u32[]{:S(2)}, u32[]{:S(2)}) %collective-permute-start.31) | collective-permute-done | bytes 32800 | tf_op jit(solution)/shard_map/ppermute | solution.py:15
  360.1 10.0 %fusion = f32[4,16,128]{2,1,0:T(8,128)} fusion(f32[4,16,128]{2,1,0:T(8,128)S(1)} %copy-done.1, f32[4,32,128,128]{3,2,1,0:T(8,128)} %param.12, f32[4,32,16,128]{3,2,1,0:T(8,128)S(1)} %bitcast.253, pred[4,32]{1,0:T(4,128)(4,1)S(1)} %get-tuple-element.14), kind=kOutput, calls=%fused_computation.7 | convolution fusion | flops 402923520 | bytes 9502848 | tf_op jit(solution)/shard_map/ikab,ikcb->ica/dot_general | solution.py:56
  (199 shorter events, 80.0 us)
Async XLA Ops:
  0.6 32.8 %collective-permute-start.5 = (f32[4,16,128]{2,1,0:T(8,128)}, f32[4,16,128]{2,1,0:T(8,128)S(1)}, u32[]{:S(2)}, u32[]{:S(2)}) collective-permute-start(f32[4,16,128]{2,1,0:T(8,128)} %param.15), channel_id=1, source_target_pairs={{3,0},{4,1},{5,2},{6,3},{7,4},{8,5},{9,6},{10,7},{11,8},{12,9},{13... | collective-permute-start | bytes 98312 | tf_op jit(solution)/shard_map/ppermute | solution.py:15
  7.4 26.0 %collective-permute-start.4 = (f32[4,16,128]{2,1,0:T(8,128)}, f32[4,16,128]{2,1,0:T(8,128)S(1)}, u32[]{:S(2)}, u32[]{:S(2)}) collective-permute-start(f32[4,16,128]{2,1,0:T(8,128)} %param.15), channel_id=1, source_target_pairs={{2,0},{3,1},{4,2},{5,3},{6,4},{7,5},{8,6},{9,7},{10,8},{11,9},{12,... | collective-permute-start | bytes 98312 | tf_op jit(solution)/shard_map/ppermute | solution.py:15
  9.5 23.9 %collective-permute-start.3 = (f32[4,16,128]{2,1,0:T(8,128)}, f32[4,16,128]{2,1,0:T(8,128)S(1)}, u32[]{:S(2)}, u32[]{:S(2)}) collective-permute-start(f32[4,16,128]{2,1,0:T(8,128)} %param.15), channel_id=1, source_target_pairs={{1,0},{2,1},{3,2},{4,3},{5,4},{6,5},{7,6},{8,7},{9,8},{10,9},{11,1... | collective-permute-start | bytes 98312 | tf_op jit(solution)/shard_map/ppermute | solution.py:15
  11.7 20.9 %collective-permute-start.2 = (f32[4,16,128]{2,1,0:T(8,128)}, f32[4,16,128]{2,1,0:T(8,128)S(1)}, u32[]{:S(2)}, u32[]{:S(2)}) collective-permute-start(f32[4,16,128]{2,1,0:T(8,128)} %param.15), channel_id=1, source_target_pairs={{0,1},{1,2},{2,3},{3,4},{4,5},{5,6},{6,7},{7,8},{8,9},{9,10},{10,1... | collective-permute-start | bytes 98312 | tf_op jit(solution)/shard_map/ppermute | solution.py:15
  15.1 9.0 %collective-permute-start = (f32[4,16,128]{2,1,0:T(8,128)}, f32[4,16,128]{2,1,0:T(8,128)S(1)}, u32[]{:S(2)}, u32[]{:S(2)}) collective-permute-start(f32[4,16,128]{2,1,0:T(8,128)} %param.15), channel_id=1, source_target_pairs={{0,3},{1,4},{2,5},{3,6},{4,7},{5,8},{6,9},{7,10},{8,11},{9,12},{10... | collective-permute-start | bytes 98312 | tf_op jit(solution)/shard_map/ppermute | solution.py:15
  24.2 8.5 %collective-permute-start.1 = (f32[4,16,128]{2,1,0:T(8,128)}, f32[4,16,128]{2,1,0:T(8,128)S(1)}, u32[]{:S(2)}, u32[]{:S(2)}) collective-permute-start(f32[4,16,128]{2,1,0:T(8,128)} %param.15), channel_id=1, source_target_pairs={{0,2},{1,3},{2,4},{3,5},{4,6},{5,7},{6,8},{7,9},{8,10},{9,11},{10,... | collective-permute-start | bytes 98312 | tf_op jit(solution)/shard_map/ppermute | solution.py:15
  90.4 19.8 %collective-permute-start.6 = (f32[4,16,128]{2,1,0:T(8,128)S(1)}, f32[4,16,128]{2,1,0:T(8,128)S(1)}, u32[]{:S(2)}, u32[]{:S(2)}) collective-permute-start(f32[4,16,128]{2,1,0:T(8,128)S(1)} %fusion.7), channel_id=1, source_target_pairs={{0,3},{1,4},{2,5},{3,6},{4,7},{5,8},{6,9},{7,10},{8,11},{9,12},{10... | collective-permute-start | bytes 98312 | tf_op jit(solution)/shard_map/ppermute | solution.py:15
  96.9 21.6 %collective-permute-start.11 = (f32[4,16,128]{2,1,0:T(8,128)S(1)}, f32[4,16,128]{2,1,0:T(8,128)S(1)}, u32[]{:S(2)}, u32[]{:S(2)}) collective-permute-start(f32[4,16,128]{2,1,0:T(8,128)S(1)} %fusion.7), channel_id=1, source_target_pairs={{3,0},{4,1},{5,2},{6,3},{7,4},{8,5},{9,6},{10,7},{11,8},{12,9},{13... | collective-permute-start | bytes 98312 | tf_op jit(solution)/shard_map/ppermute | solution.py:15
  99.8 18.7 %collective-permute-start.10 = (f32[4,16,128]{2,1,0:T(8,128)S(1)}, f32[4,16,128]{2,1,0:T(8,128)S(1)}, u32[]{:S(2)}, u32[]{:S(2)}) collective-permute-start(f32[4,16,128]{2,1,0:T(8,128)S(1)} %fusion.7), channel_id=1, source_target_pairs={{2,0},{3,1},{4,2},{5,3},{6,4},{7,5},{8,6},{9,7},{10,8},{11,9},{12,... | collective-permute-start | bytes 98312 | tf_op jit(solution)/shard_map/ppermute | solution.py:15
  104.6 13.9 %collective-permute-start.9 = (f32[4,16,128]{2,1,0:T(8,128)S(1)}, f32[4,16,128]{2,1,0:T(8,128)S(1)}, u32[]{:S(2)}, u32[]{:S(2)}) collective-permute-start(f32[4,16,128]{2,1,0:T(8,128)S(1)} %fusion.7), channel_id=1, source_target_pairs={{1,0},{2,1},{3,2},{4,3},{5,4},{6,5},{7,6},{8,7},{9,8},{10,9},{11,1... | collective-permute-start | bytes 98312 | tf_op jit(solution)/shard_map/ppermute | solution.py:15
  106.5 11.9 %collective-permute-start.8 = (f32[4,16,128]{2,1,0:T(8,128)S(1)}, f32[4,16,128]{2,1,0:T(8,128)S(1)}, u32[]{:S(2)}, u32[]{:S(2)}) collective-permute-start(f32[4,16,128]{2,1,0:T(8,128)S(1)} %fusion.7), channel_id=1, source_target_pairs={{0,1},{1,2},{2,3},{3,4},{4,5},{5,6},{6,7},{7,8},{8,9},{9,10},{10,1... | collective-permute-start | bytes 98312 | tf_op jit(solution)/shard_map/ppermute | solution.py:15
  169.7 19.9 %collective-permute-start.12 = (f32[4,16,128]{2,1,0:T(8,128)S(1)}, f32[4,16,128]{2,1,0:T(8,128)S(1)}, u32[]{:S(2)}, u32[]{:S(2)}) collective-permute-start(f32[4,16,128]{2,1,0:T(8,128)S(1)} %fusion.6), channel_id=1, source_target_pairs={{0,3},{1,4},{2,5},{3,6},{4,7},{5,8},{6,9},{7,10},{8,11},{9,12},{10... | collective-permute-start | bytes 98312 | tf_op jit(solution)/shard_map/ppermute | solution.py:15
  176.4 21.6 %collective-permute-start.17 = (f32[4,16,128]{2,1,0:T(8,128)S(1)}, f32[4,16,128]{2,1,0:T(8,128)S(1)}, u32[]{:S(2)}, u32[]{:S(2)}) collective-permute-start(f32[4,16,128]{2,1,0:T(8,128)S(1)} %fusion.6), channel_id=1, source_target_pairs={{3,0},{4,1},{5,2},{6,3},{7,4},{8,5},{9,6},{10,7},{11,8},{12,9},{13... | collective-permute-start | bytes 98312 | tf_op jit(solution)/shard_map/ppermute | solution.py:15
  179.6 18.4 %collective-permute-start.16 = (f32[4,16,128]{2,1,0:T(8,128)S(1)}, f32[4,16,128]{2,1,0:T(8,128)S(1)}, u32[]{:S(2)}, u32[]{:S(2)}) collective-permute-start(f32[4,16,128]{2,1,0:T(8,128)S(1)} %fusion.6), channel_id=1, source_target_pairs={{2,0},{3,1},{4,2},{5,3},{6,4},{7,5},{8,6},{9,7},{10,8},{11,9},{12,... | collective-permute-start | bytes 98312 | tf_op jit(solution)/shard_map/ppermute | solution.py:15
  184.0 13.9 %collective-permute-start.15 = (f32[4,16,128]{2,1,0:T(8,128)S(1)}, f32[4,16,128]{2,1,0:T(8,128)S(1)}, u32[]{:S(2)}, u32[]{:S(2)}) collective-permute-start(f32[4,16,128]{2,1,0:T(8,128)S(1)} %fusion.6), channel_id=1, source_target_pairs={{1,0},{2,1},{3,2},{4,3},{5,4},{6,5},{7,6},{8,7},{9,8},{10,9},{11,1... | collective-permute-start | bytes 98312 | tf_op jit(solution)/shard_map/ppermute | solution.py:15
  186.0 11.9 %collective-permute-start.14 = (f32[4,16,128]{2,1,0:T(8,128)S(1)}, f32[4,16,128]{2,1,0:T(8,128)S(1)}, u32[]{:S(2)}, u32[]{:S(2)}) collective-permute-start(f32[4,16,128]{2,1,0:T(8,128)S(1)} %fusion.6), channel_id=1, source_target_pairs={{0,1},{1,2},{2,3},{3,4},{4,5},{5,6},{6,7},{7,8},{8,9},{9,10},{10,1... | collective-permute-start | bytes 98312 | tf_op jit(solution)/shard_map/ppermute | solution.py:15
  208.7 10.1 %collective-permute-start.18 = (f32[4,16,128]{2,1,0:T(8,128)S(1)}, f32[4,16,128]{2,1,0:T(8,128)S(1)}, u32[]{:S(2)}, u32[]{:S(2)}) collective-permute-start(f32[4,16,128]{2,1,0:T(8,128)S(1)} %fusion.85), channel_id=1, source_target_pairs={{0,3},{1,4},{2,5},{3,6},{4,7},{8,11},{9,12},{10,13},{11,14},{12,15... | collective-permute-start | bytes 98312 | tf_op jit(solution)/shard_map/ppermute | solution.py:15
  210.2 13.7 %collective-permute-start.23 = (f32[4,16,128]{2,1,0:T(8,128)S(1)}, f32[4,16,128]{2,1,0:T(8,128)S(1)}, u32[]{:S(2)}, u32[]{:S(2)}) collective-permute-start(f32[4,16,128]{2,1,0:T(8,128)S(1)} %fusion.85), channel_id=1, source_target_pairs={{3,0},{4,1},{5,2},{6,3},{7,4},{11,8},{12,9},{13,10},{14,11},{15,12... | collective-permute-start | bytes 98312 | tf_op jit(solution)/shard_map/ppermute | solution.py:15
  211.5 12.4 %collective-permute-start.22 = (f32[4,16,128]{2,1,0:T(8,128)S(1)}, f32[4,16,128]{2,1,0:T(8,128)S(1)}, u32[]{:S(2)}, u32[]{:S(2)}) collective-permute-start(f32[4,16,128]{2,1,0:T(8,128)S(1)} %fusion.85), channel_id=1, source_target_pairs={{2,0},{3,1},{4,2},{5,3},{6,4},{7,5},{10,8},{11,9},{12,10},{13,11},... | collective-permute-start | bytes 98312 | tf_op jit(solution)/shard_map/ppermute | solution.py:15
  212.8 11.1 %collective-permute-start.21 = (f32[4,16,128]{2,1,0:T(8,128)S(1)}, f32[4,16,128]{2,1,0:T(8,128)S(1)}, u32[]{:S(2)}, u32[]{:S(2)}) collective-permute-start(f32[4,16,128]{2,1,0:T(8,128)S(1)} %fusion.85), channel_id=1, source_target_pairs={{1,0},{2,1},{3,2},{4,3},{5,4},{6,5},{7,6},{9,8},{10,9},{11,10},{12... | collective-permute-start | bytes 98312 | tf_op jit(solution)/shard_map/ppermute | solution.py:15
  214.7 9.1 %collective-permute-start.20 = (f32[4,16,128]{2,1,0:T(8,128)S(1)}, f32[4,16,128]{2,1,0:T(8,128)S(1)}, u32[]{:S(2)}, u32[]{:S(2)}) collective-permute-start(f32[4,16,128]{2,1,0:T(8,128)S(1)} %fusion.85), channel_id=1, source_target_pairs={{0,1},{1,2},{2,3},{3,4},{4,5},{5,6},{6,7},{8,9},{9,10},{10,11},{11... | collective-permute-start | bytes 98312 | tf_op jit(solution)/shard_map/ppermute | solution.py:15
  286.6 10.9 %collective-permute-start.24 = (f32[4,16,128]{2,1,0:T(8,128)S(1)}, f32[4,16,128]{2,1,0:T(8,128)S(1)}, u32[]{:S(2)}, u32[]{:S(2)}) collective-permute-start(f32[4,16,128]{2,1,0:T(8,128)S(1)} %fusion.3), channel_id=1, source_target_pairs={{0,3},{1,4},{2,5},{3,6},{4,7},{8,11},{9,12},{10,13},{11,14},{12,15... | collective-permute-start | bytes 98312 | tf_op jit(solution)/shard_map/ppermute | solution.py:15
  288.1 14.6 %collective-permute-start.29 = (f32[4,16,128]{2,1,0:T(8,128)S(1)}, f32[4,16,128]{2,1,0:T(8,128)S(1)}, u32[]{:S(2)}, u32[]{:S(2)}) collective-permute-start(f32[4,16,128]{2,1,0:T(8,128)S(1)} %fusion.3), channel_id=1, source_target_pairs={{3,0},{4,1},{5,2},{6,3},{7,4},{11,8},{12,9},{13,10},{14,11},{15,12... | collective-permute-start | bytes 98312 | tf_op jit(solution)/shard_map/ppermute | solution.py:15
  289.4 13.2 %collective-permute-start.28 = (f32[4,16,128]{2,1,0:T(8,128)S(1)}, f32[4,16,128]{2,1,0:T(8,128)S(1)}, u32[]{:S(2)}, u32[]{:S(2)}) collective-permute-start(f32[4,16,128]{2,1,0:T(8,128)S(1)} %fusion.3), channel_id=1, source_target_pairs={{2,0},{3,1},{4,2},{5,3},{6,4},{7,5},{10,8},{11,9},{12,10},{13,11},... | collective-permute-start | bytes 98312 | tf_op jit(solution)/shard_map/ppermute | solution.py:15
  290.7 11.9 %collective-permute-start.27 = (f32[4,16,128]{2,1,0:T(8,128)S(1)}, f32[4,16,128]{2,1,0:T(8,128)S(1)}, u32[]{:S(2)}, u32[]{:S(2)}) collective-permute-start(f32[4,16,128]{2,1,0:T(8,128)S(1)} %fusion.3), channel_id=1, source_target_pairs={{1,0},{2,1},{3,2},{4,3},{5,4},{6,5},{7,6},{9,8},{10,9},{11,10},{12... | collective-permute-start | bytes 98312 | tf_op jit(solution)/shard_map/ppermute | solution.py:15
  293.4 9.2 %collective-permute-start.26 = (f32[4,16,128]{2,1,0:T(8,128)S(1)}, f32[4,16,128]{2,1,0:T(8,128)S(1)}, u32[]{:S(2)}, u32[]{:S(2)}) collective-permute-start(f32[4,16,128]{2,1,0:T(8,128)S(1)} %fusion.3), channel_id=1, source_target_pairs={{0,1},{1,2},{2,3},{3,4},{4,5},{5,6},{6,7},{8,9},{9,10},{10,11},{11... | collective-permute-start | bytes 98312 | tf_op jit(solution)/shard_map/ppermute | solution.py:15
  331.7 18.6 %collective-permute-start.30 = (f32[4,16,128]{2,1,0:T(8,128)S(1)}, f32[4,16,128]{2,1,0:T(8,128)S(1)}, u32[]{:S(2)}, u32[]{:S(2)}) collective-permute-start(f32[4,16,128]{2,1,0:T(8,128)S(1)} %fusion.2), channel_id=1, source_target_pairs={{0,3},{1,4},{2,5},{3,6},{4,7},{5,8},{6,9},{7,10},{8,11},{9,12},{10... | collective-permute-start | bytes 98312 | tf_op jit(solution)/shard_map/ppermute | solution.py:15
  333.6 25.7 %collective-permute-start.35 = (f32[4,16,128]{2,1,0:T(8,128)S(1)}, f32[4,16,128]{2,1,0:T(8,128)S(1)}, u32[]{:S(2)}, u32[]{:S(2)}) collective-permute-start(f32[4,16,128]{2,1,0:T(8,128)S(1)} %fusion.2), channel_id=1, source_target_pairs={{3,0},{4,1},{5,2},{6,3},{7,4},{8,5},{9,6},{10,7},{11,8},{12,9},{13... | collective-permute-start | bytes 98312 | tf_op jit(solution)/shard_map/ppermute | solution.py:15
  340.9 18.4 %collective-permute-start.34 = (f32[4,16,128]{2,1,0:T(8,128)S(1)}, f32[4,16,128]{2,1,0:T(8,128)S(1)}, u32[]{:S(2)}, u32[]{:S(2)}) collective-permute-start(f32[4,16,128]{2,1,0:T(8,128)S(1)} %fusion.2), channel_id=1, source_target_pairs={{2,0},{3,1},{4,2},{5,3},{6,4},{7,5},{8,6},{9,7},{10,8},{11,9},{12,... | collective-permute-start | bytes 98312 | tf_op jit(solution)/shard_map/ppermute | solution.py:15
  342.8 16.4 %collective-permute-start.33 = (f32[4,16,128]{2,1,0:T(8,128)S(1)}, f32[4,16,128]{2,1,0:T(8,128)S(1)}, u32[]{:S(2)}, u32[]{:S(2)}) collective-permute-start(f32[4,16,128]{2,1,0:T(8,128)S(1)} %fusion.2), channel_id=1, source_target_pairs={{1,0},{2,1},{3,2},{4,3},{5,4},{6,5},{7,6},{8,7},{9,8},{10,9},{11,1... | collective-permute-start | bytes 98312 | tf_op jit(solution)/shard_map/ppermute | solution.py:15
  346.8 12.4 %collective-permute-start.32 = (f32[4,16,128]{2,1,0:T(8,128)S(1)}, f32[4,16,128]{2,1,0:T(8,128)S(1)}, u32[]{:S(2)}, u32[]{:S(2)}) collective-permute-start(f32[4,16,128]{2,1,0:T(8,128)S(1)} %fusion.2), channel_id=1, source_target_pairs={{0,1},{1,2},{2,3},{3,4},{4,5},{5,6},{6,7},{7,8},{8,9},{9,10},{10,1... | collective-permute-start | bytes 98312 | tf_op jit(solution)/shard_map/ppermute | solution.py:15
  350.3 8.9 %collective-permute-start.31 = (f32[4,16,128]{2,1,0:T(8,128)S(1)}, f32[4,16,128]{2,1,0:T(8,128)S(1)}, u32[]{:S(2)}, u32[]{:S(2)}) collective-permute-start(f32[4,16,128]{2,1,0:T(8,128)S(1)} %fusion.2), channel_id=1, source_target_pairs={{0,2},{1,3},{2,4},{3,5},{4,6},{5,7},{6,8},{7,9},{8,10},{9,11},{10,... | collective-permute-start | bytes 98312 | tf_op jit(solution)/shard_map/ppermute | solution.py:15
  (8 other events, 354.3 us)
where the time goes:
time: 372 us; the launch traced here: 370 us
  blocking collectives  128 us (34%)
  starting transfers between devices  113 us (30%)
  matrix products  64.6 us (17%)
  waiting for transfers between devices  30.9 us (8%)
  other arithmetic  24.9 us (7%)
  local copies, waits for them, and re-layouts  6.56 us (2%)
    ppermute x36, starting transfers between devices, from_behind(): lax.ppermute(value, axis, [(source, source + steps) for source in range(f...  113 us
    dot_general x6, matrix products, tile_product(): jnp.einsum('ikab,ikcb->ica', matrix_tiles, picked, precision=lax.Precisio...  57 us
    psum x1, blocking collectives, per_device(): lax.psum((inner_products(direction, applied), inner_products(applied, res...  36.1 us
    psum x1, blocking collectives, per_device(): squares = lax.psum(inner_products(residual, residual), ('grp', 'row'))  36.1 us
    ppermute x36, waiting for transfers between devices, from_behind(): lax.ppermute(value, axis, [(source, source + steps) for source in range(f...  30.9 us
    psum x1, blocking collectives, per_device(): weight = lax.psum(inner_products(remainder, smoothed), 'row')  24.9 us
    psum x1, blocking collectives, per_device(): weight_next = lax.psum(inner_products(remainder, smoothed), 'row')  17.3 us
    psum x1, blocking collectives, per_device(): bending = lax.psum(inner_products(heading, applied), 'row')  13.9 us
  transfers between devices with their start and end apart: 36, of which 7 were waited for; matrix products, arithmetic and copies ran while one was open for 1% of the time, Pallas kernels for 0%

commit v1 on v0

--- a/solution.py
+++ b/solution.py
@@ -74,7 +74,9 @@
     solution = jnp.zeros_like(right_side)
     residual = right_side
     direction = right_side
-    squares = lax.psum(inner_products(residual, residual), ("grp", "row"))
+    squares = inner_products(residual, residual)
+    for mesh_axis in ("row", "grp"):
+        squares = lax.psum(squares, mesh_axis)
     for outer_step in range(OUTER):
         applied = full_product(direction)
         curvature, crossed, square = lax.psum(

time: 372 us -> 393 us (1.056)
  blocking collectives: 128 us -> 155 us
  waiting for transfers between devices: 30.9 us -> 26.5 us
    psum x1 -> x2, blocking collectives: 36.1 us -> 78.2 us  [per_device(): lax.psum((inner_products(direction, applied), inner_products(applied, res...]
    psum x1 -> x2, blocking collectives: 36.1 us -> 20.9 us  [per_device(): squares = lax.psum(squares, mesh_axis)]
    ppermute x36, waiting for transfers between devices: 30.9 us -> 26.5 us  [from_behind(): lax.ppermute(value, axis, [(source, source + steps) for source in range(f...]
  transfers between devices with their start and end apart: 36 -> 36, of which waited for: 7 -> 6; matrix products, arithmetic and copies ran while one was open for 1% -> 2% of each run, Pallas kernels for 0% -> 0%
where the time goes in v1:
time: 393 us; the launch traced here: 392 us
  blocking collectives  155 us (39%)
  starting transfers between devices  112 us (28%)
  matrix products  64.6 us (16%)
  waiting for transfers between devices  26.5 us (7%)
  other arithmetic  24.9 us (6%)
  local copies, waits for them, and re-layouts  6.56 us (2%)
    ppermute x36, starting transfers between devices, from_behind(): lax.ppermute(value, axis, [(source, source + steps) for source in range(f...  112 us
    psum x2, blocking collectives, per_device(): lax.psum((inner_products(direction, applied), inner_products(applied, res...  78.2 us
    dot_general x6, matrix products, tile_product(): jnp.einsum('ikab,ikcb->ica', matrix_tiles, picked, precision=lax.Precisio...  57 us
    ppermute x36, waiting for transfers between devices, from_behind(): lax.ppermute(value, axis, [(source, source + steps) for source in range(f...  26.5 us
    psum x1, blocking collectives, per_device(): weight = lax.psum(inner_products(remainder, smoothed), 'row')  24.9 us
    psum x2, blocking collectives, per_device(): squares = lax.psum(squares, mesh_axis)  20.9 us
    psum x1, blocking collectives, per_device(): weight_next = lax.psum(inner_products(remainder, smoothed), 'row')  17.3 us
    psum x1, blocking collectives, per_device(): bending = lax.psum(inner_products(heading, applied), 'row')  13.9 us
  transfers between devices with their start and end apart: 36, of which 6 were waited for; matrix products, arithmetic and copies ran while one was open for 2% of the time, Pallas kernels for 0%

profile of v1, /device:TPU:5, one launch (start us, length us, event | category | flops | bytes accessed | tf_op | source)
XLA Modules:
  0.0 391.6 jit_solution(1725631330179012455)
XLA Ops:
  0.6 6.8 %collective-permute-start.5 = (f32[4,16,128]{2,1,0:T(8,128)}, f32[4,16,128]{2,1,0:T(8,128)S(1)}, u32[]{:S(2)}, u32[]{:S(2)}) collective-permute-start(f32[4,16,128]{2,1,0:T(8,128)} %param.15), channel_id=1, source_target_pairs={{3,0},{4,1},{5,2},{6,3},{7,4},{8,5},{9,6},{10,7},{11,8},{12,9},{13... | collective-permute-start | bytes 98312 | tf_op jit(solution)/shard_map/ppermute | solution.py:15
  19.8 13.8 %psum.71 = f32[16,16]{1,0:T(8,128)S(1)} all-reduce(f32[16,16]{1,0:T(8,128)S(1)} %convolution_bitcast_fusion.21), channel_id=1, replica_groups=mesh['grp'=4,'row'=8] {'row'}, use_global_device_ids=true, to_apply=%region_3.6 | all-reduce | flops 256 | bytes 2048 | tf_op jit(solution)/shard_map/psum | solution.py:79
  33.6 7.1 %psum.72 = f32[16,16]{1,0:T(8,128)S(1)} all-reduce(f32[16,16]{1,0:T(8,128)S(1)} %psum.71), channel_id=1, replica_groups=mesh['grp'=4,'row'=8] {'grp'}, use_global_device_ids=true, to_apply=%region_4.7 | all-reduce | flops 256 | bytes 2048 | tf_op jit(solution)/shard_map/psum | solution.py:79
  46.9 6.5 %collective-permute-done.1 = f32[4,16,128]{2,1,0:T(8,128)S(1)} collective-permute-done((f32[4,16,128]{2,1,0:T(8,128)}, f32[4,16,128]{2,1,0:T(8,128)S(1)}, u32[]{:S(2)}, u32[]{:S(2)}) %collective-permute-start.1) | collective-permute-done | bytes 32800 | tf_op jit(solution)/shard_map/ppermute | solution.py:15
  55.0 9.4 %convolution_bitcast_fusion.9 = f32[4,16,128]{2,1,0:T(8,128)S(1)} fusion(f32[4,32,128,128]{3,2,1,0:T(8,128)} %param.12, f32[4,32,16,128]{3,2,1,0:T(8,128)S(1)} %bitcast.254, pred[4,32]{1,0:T(4,128)(4,1)S(1)} %get-tuple-element.13), kind=kOutput, calls=%fused_computation.26 | convolution fusion | flops 402915328 | bytes 9470080 | tf_op jit(solution)/shard_map/ikab,ikcb->ica/dot_general | solution.py:56
  64.8 42.0 %all-reduce = (f32[16,16]{1,0:T(8,128)S(1)}, f32[16,16]{1,0:T(8,128)S(1)}, f32[16,16]{1,0:T(8,128)S(1)}) all-reduce(f32[16,16]{1,0:T(8,128)S(1)} %bitcast.256, f32[16,16]{1,0:T(8,128)S(1)} %convolution_bitcast_fusion.22, f32[16,16]{1,0:T(8,128)S(1)} %convolution_bitcast_fusion.20), channel_id=1, replica_groups=mesh['grp'=4,'row'=8] {'grp','row'}, use_global_device_ids=true, to_apply=%region_0.2 | all-reduce | flops 768 | bytes 6144 | tf_op jit(solution)/shard_map/psum | solution.py:82
  112.9 5.4 %collective-permute-start.6 = (f32[4,16,128]{2,1,0:T(8,128)S(1)}, f32[4,16,128]{2,1,0:T(8,128)S(1)}, u32[]{:S(2)}, u32[]{:S(2)}) collective-permute-start(f32[4,16,128]{2,1,0:T(8,128)S(1)} %fusion.7), channel_id=1, source_target_pairs={{0,3},{1,4},{2,5},{3,6},{4,7},{5,8},{6,9},{7,10},{8,11},{9,12},{10... | collective-permute-start | bytes 98312 | tf_op jit(solution)/shard_map/ppermute | solution.py:15
  118.6 3.7 collective-permute-start.11
  122.3 3.8 collective-permute-start.10
  128.1 3.6 collective-permute-start.8
  134.2 5.8 %collective-permute-done.7 = f32[4,16,128]{2,1,0:T(8,128)S(1)} collective-permute-done((f32[4,16,128]{2,1,0:T(8,128)S(1)}, f32[4,16,128]{2,1,0:T(8,128)S(1)}, u32[]{:S(2)}, u32[]{:S(2)}) %collective-permute-start.7) | collective-permute-done | bytes 32800 | tf_op jit(solution)/shard_map/ppermute | solution.py:15
  140.9 9.4 %convolution_bitcast_fusion.6 = f32[4,16,128]{2,1,0:T(8,128)S(1)} fusion(f32[4,32,128,128]{3,2,1,0:T(8,128)} %param.12, f32[4,32,16,128]{3,2,1,0:T(8,128)S(1)} %bitcast.255, pred[4,32]{1,0:T(4,128)(4,1)S(1)} %get-tuple-element.13), kind=kOutput, calls=%fused_computation.21 | convolution fusion | flops 402915328 | bytes 9470080 | tf_op jit(solution)/shard_map/ikab,ikcb->ica/dot_general | solution.py:56
  150.4 36.1 %psum.75 = f32[16,16]{1,0:T(8,128)S(1)} all-reduce(f32[16,16]{1,0:T(8,128)S(1)} %convolution_bitcast_fusion.18), channel_id=1, replica_groups=mesh['grp'=4,'row'=8] {'grp','row'}, use_global_device_ids=true, to_apply=%region_7.12 | all-reduce | flops 256 | bytes 2048 | tf_op jit(solution)/shard_map/psum | solution.py:82
  191.3 6.0 %collective-permute-start.12 = (f32[4,16,128]{2,1,0:T(8,128)S(1)}, f32[4,16,128]{2,1,0:T(8,128)S(1)}, u32[]{:S(2)}, u32[]{:S(2)}) collective-permute-start(f32[4,16,128]{2,1,0:T(8,128)S(1)} %fusion.6), channel_id=1, source_target_pairs={{0,3},{1,4},{2,5},{3,6},{4,7},{5,8},{6,9},{7,10},{8,11},{9,12},{10... | collective-permute-start | bytes 98312 | tf_op jit(solution)/shard_map/ppermute | solution.py:15
  201.2 4.4 %collective-permute-start.16 = (f32[4,16,128]{2,1,0:T(8,128)S(1)}, f32[4,16,128]{2,1,0:T(8,128)S(1)}, u32[]{:S(2)}, u32[]{:S(2)}) collective-permute-start(f32[4,16,128]{2,1,0:T(8,128)S(1)} %fusion.6), channel_id=1, source_target_pairs={{2,0},{3,1},{4,2},{5,3},{6,4},{7,5},{8,6},{9,7},{10,8},{11,9},{12,... | collective-permute-start | bytes 98312 | tf_op jit(solution)/shard_map/ppermute | solution.py:15
  207.6 3.6 collective-permute-start.14
  213.9 5.6 %collective-permute-done.13 = f32[4,16,128]{2,1,0:T(8,128)S(1)} collective-permute-done((f32[4,16,128]{2,1,0:T(8,128)S(1)}, f32[4,16,128]{2,1,0:T(8,128)S(1)}, u32[]{:S(2)}, u32[]{:S(2)}) %collective-permute-start.13) | collective-permute-done | bytes 32800 | tf_op jit(solution)/shard_map/ppermute | solution.py:15
  220.3 9.4 %fusion.5 = f32[4,16,128]{2,1,0:T(8,128)S(1)} fusion(f32[4,16,128]{2,1,0:T(8,128)S(1)} %copy-done.1, f32[4,32,128,128]{3,2,1,0:T(8,128)} %param.12, f32[4,32,16,128]{3,2,1,0:T(8,128)S(1)} %bitcast.250, f32[4,32]{1,0:T(4,128)S(1)} %get-tuple-element.12, pred[4,32]{1,0:T(4,128)(4,1)S(1)} %get-tuple-element.13), kind=kOutput, calls=%fused_computation.18 | convolution fusion | flops 403185664 | bytes 9503360 | tf_op jit(solution)/shard_map/ikab,ikcb->ica/dot_general | solution.py:56
  236.3 4.1 %collective-permute-start.20 = (f32[4,16,128]{2,1,0:T(8,128)S(1)}, f32[4,16,128]{2,1,0:T(8,128)S(1)}, u32[]{:S(2)}, u32[]{:S(2)}) collective-permute-start(f32[4,16,128]{2,1,0:T(8,128)S(1)} %fusion.85), channel_id=1, source_target_pairs={{0,1},{1,2},{2,3},{3,4},{4,5},{5,6},{6,7},{8,9},{9,10},{10,11},{11... | collective-permute-start | bytes 98312 | tf_op jit(solution)/shard_map/ppermute | solution.py:15
  240.4 4.0 %collective-permute-start.19 = (f32[4,16,128]{2,1,0:T(8,128)S(1)}, f32[4,16,128]{2,1,0:T(8,128)S(1)}, u32[]{:S(2)}, u32[]{:S(2)}) collective-permute-start(f32[4,16,128]{2,1,0:T(8,128)S(1)} %fusion.85), channel_id=1, source_target_pairs={{0,2},{1,3},{2,4},{3,5},{4,6},{5,7},{8,10},{9,11},{10,12},{11,13},... | collective-permute-start | bytes 98312 | tf_op jit(solution)/shard_map/ppermute | solution.py:15
  246.2 9.4 %convolution_bitcast_fusion.4 = f32[4,16,128]{2,1,0:T(8,128)S(1)} fusion(f32[4,32,128,128]{3,2,1,0:T(8,128)} %param.12, f32[4,32,16,128]{3,2,1,0:T(8,128)S(1)} %bitcast.251, f32[4,32]{1,0:T(4,128)S(1)} %get-tuple-element.11, pred[4,32]{1,0:T(4,128)(4,1)S(1)} %get-tuple-element.13), kind=kOutput, calls=%fused_computation.16 | convolution fusion | flops 403177472 | bytes 9470592 | tf_op jit(solution)/shard_map/ikab,ikcb->ica/dot_general | solution.py:56
  255.8 24.9 %all-reduce.1 = (f32[16,16]{1,0:T(8,128)S(1)}, f32[16,16]{1,0:T(8,128)S(1)}) all-reduce(f32[16,16]{1,0:T(8,128)S(1)} %convolution_bitcast_fusion.15, f32[16,16]{1,0:T(8,128)S(1)} %convolution_bitcast_fusion.16), channel_id=1, replica_groups=mesh['grp'=4,'row'=8] {'row'}, use_global_device_ids=true, to_apply=%region_9.14 | all-reduce | flops 512 | bytes 4096 | tf_op jit(solution)/shard_map/psum | solution.py:112
  290.3 17.3 %psum.78 = f32[16,16]{1,0:T(8,128)S(1)} all-reduce(f32[16,16]{1,0:T(8,128)S(1)} %convolution_bitcast_fusion.13), channel_id=1, replica_groups=mesh['grp'=4,'row'=8] {'row'}, use_global_device_ids=true, to_apply=%region_10.15 | all-reduce | flops 256 | bytes 2048 | tf_op jit(solution)/shard_map/psum | solution.py:123
  314.9 4.2 %collective-permute-start.26 = (f32[4,16,128]{2,1,0:T(8,128)S(1)}, f32[4,16,128]{2,1,0:T(8,128)S(1)}, u32[]{:S(2)}, u32[]{:S(2)}) collective-permute-start(f32[4,16,128]{2,1,0:T(8,128)S(1)} %fusion.3), channel_id=1, source_target_pairs={{0,1},{1,2},{2,3},{3,4},{4,5},{5,6},{6,7},{8,9},{9,10},{10,11},{11... | collective-permute-start | bytes 98312 | tf_op jit(solution)/shard_map/ppermute | solution.py:15
  319.1 4.2 %collective-permute-start.25 = (f32[4,16,128]{2,1,0:T(8,128)S(1)}, f32[4,16,128]{2,1,0:T(8,128)S(1)}, u32[]{:S(2)}, u32[]{:S(2)}) collective-permute-start(f32[4,16,128]{2,1,0:T(8,128)S(1)} %fusion.3), channel_id=1, source_target_pairs={{0,2},{1,3},{2,4},{3,5},{4,6},{5,7},{8,10},{9,11},{10,12},{11,13},... | collective-permute-start | bytes 98312 | tf_op jit(solution)/shard_map/ppermute | solution.py:15
  325.0 9.4 %convolution_bitcast_fusion.1 = f32[4,16,128]{2,1,0:T(8,128)S(1)} fusion(f32[4,32,128,128]{3,2,1,0:T(8,128)} %param.12, f32[4,32,16,128]{3,2,1,0:T(8,128)S(1)} %bitcast.252, f32[4,32]{1,0:T(4,128)S(1)} %get-tuple-element.11, pred[4,32]{1,0:T(4,128)(4,1)S(1)} %get-tuple-element.13), kind=kOutput, calls=%fused_computation.11 | convolution fusion | flops 403177472 | bytes 9470592 | tf_op jit(solution)/shard_map/ikab,ikcb->ica/dot_general | solution.py:56
  334.5 13.9 %psum.79 = f32[16,16]{1,0:T(8,128)S(1)} all-reduce(f32[16,16]{1,0:T(8,128)S(1)} %convolution_bitcast_fusion.11), channel_id=1, replica_groups=mesh['grp'=4,'row'=8] {'row'}, use_global_device_ids=true, to_apply=%region_11.16 | all-reduce | flops 256 | bytes 2048 | tf_op jit(solution)/shard_map/psum | solution.py:117
  355.2 7.2 %collective-permute-start.35 = (f32[4,16,128]{2,1,0:T(8,128)S(1)}, f32[4,16,128]{2,1,0:T(8,128)S(1)}, u32[]{:S(2)}, u32[]{:S(2)}) collective-permute-start(f32[4,16,128]{2,1,0:T(8,128)S(1)} %fusion.2), channel_id=1, source_target_pairs={{3,0},{4,1},{5,2},{6,3},{7,4},{8,5},{9,6},{10,7},{11,8},{12,9},{13... | collective-permute-start | bytes 98312 | tf_op jit(solution)/shard_map/ppermute | solution.py:15
  364.4 4.0 %collective-permute-start.33 = (f32[4,16,128]{2,1,0:T(8,128)S(1)}, f32[4,16,128]{2,1,0:T(8,128)S(1)}, u32[]{:S(2)}, u32[]{:S(2)}) collective-permute-start(f32[4,16,128]{2,1,0:T(8,128)S(1)} %fusion.2), channel_id=1, source_target_pairs={{1,0},{2,1},{3,2},{4,3},{5,4},{6,5},{7,6},{8,7},{9,8},{10,9},{11,1... | collective-permute-start | bytes 98312 | tf_op jit(solution)/shard_map/ppermute | solution.py:15
  368.3 3.5 collective-permute-start.32
  373.9 6.8 %collective-permute-done.31 = f32[4,16,128]{2,1,0:T(8,128)S(1)} collective-permute-done((f32[4,16,128]{2,1,0:T(8,128)S(1)}, f32[4,16,128]{2,1,0:T(8,128)S(1)}, u32[]{:S(2)}, u32[]{:S(2)}) %collective-permute-start.31) | collective-permute-done | bytes 32800 | tf_op jit(solution)/shard_map/ppermute | solution.py:15
  381.6 10.0 %fusion = f32[4,16,128]{2,1,0:T(8,128)} fusion(f32[4,16,128]{2,1,0:T(8,128)S(1)} %copy-done.1, f32[4,32,128,128]{3,2,1,0:T(8,128)} %param.12, f32[4,32,16,128]{3,2,1,0:T(8,128)S(1)} %bitcast.253, pred[4,32]{1,0:T(4,128)(4,1)S(1)} %get-tuple-element.13), kind=kOutput, calls=%fused_computation.7 | convolution fusion | flops 402923520 | bytes 9502848 | tf_op jit(solution)/shard_map/ikab,ikcb->ica/dot_general | solution.py:56
  (201 shorter events, 83.8 us)
Async XLA Ops:
  0.6 53.6 %collective-permute-start.5 = (f32[4,16,128]{2,1,0:T(8,128)}, f32[4,16,128]{2,1,0:T(8,128)S(1)}, u32[]{:S(2)}, u32[]{:S(2)}) collective-permute-start(f32[4,16,128]{2,1,0:T(8,128)} %param.15), channel_id=1, source_target_pairs={{3,0},{4,1},{5,2},{6,3},{7,4},{8,5},{9,6},{10,7},{11,8},{12,9},{13... | collective-permute-start | bytes 98312 | tf_op jit(solution)/shard_map/ppermute | solution.py:15
  7.4 46.7 %collective-permute-start.4 = (f32[4,16,128]{2,1,0:T(8,128)}, f32[4,16,128]{2,1,0:T(8,128)S(1)}, u32[]{:S(2)}, u32[]{:S(2)}) collective-permute-start(f32[4,16,128]{2,1,0:T(8,128)} %param.15), channel_id=1, source_target_pairs={{2,0},{3,1},{4,2},{5,3},{6,4},{7,5},{8,6},{9,7},{10,8},{11,9},{12,... | collective-permute-start | bytes 98312 | tf_op jit(solution)/shard_map/ppermute | solution.py:15
  9.5 44.6 %collective-permute-start.3 = (f32[4,16,128]{2,1,0:T(8,128)}, f32[4,16,128]{2,1,0:T(8,128)S(1)}, u32[]{:S(2)}, u32[]{:S(2)}) collective-permute-start(f32[4,16,128]{2,1,0:T(8,128)} %param.15), channel_id=1, source_target_pairs={{1,0},{2,1},{3,2},{4,3},{5,4},{6,5},{7,6},{8,7},{9,8},{10,9},{11,1... | collective-permute-start | bytes 98312 | tf_op jit(solution)/shard_map/ppermute | solution.py:15
  11.7 41.7 %collective-permute-start.2 = (f32[4,16,128]{2,1,0:T(8,128)}, f32[4,16,128]{2,1,0:T(8,128)S(1)}, u32[]{:S(2)}, u32[]{:S(2)}) collective-permute-start(f32[4,16,128]{2,1,0:T(8,128)} %param.15), channel_id=1, source_target_pairs={{0,1},{1,2},{2,3},{3,4},{4,5},{5,6},{6,7},{7,8},{8,9},{9,10},{10,1... | collective-permute-start | bytes 98312 | tf_op jit(solution)/shard_map/ppermute | solution.py:15
  15.1 29.8 %collective-permute-start = (f32[4,16,128]{2,1,0:T(8,128)}, f32[4,16,128]{2,1,0:T(8,128)S(1)}, u32[]{:S(2)}, u32[]{:S(2)}) collective-permute-start(f32[4,16,128]{2,1,0:T(8,128)} %param.15), channel_id=1, source_target_pairs={{0,3},{1,4},{2,5},{3,6},{4,7},{5,8},{6,9},{7,10},{8,11},{9,12},{10... | collective-permute-start | bytes 98312 | tf_op jit(solution)/shard_map/ppermute | solution.py:15
  44.9 8.5 %collective-permute-start.1 = (f32[4,16,128]{2,1,0:T(8,128)}, f32[4,16,128]{2,1,0:T(8,128)S(1)}, u32[]{:S(2)}, u32[]{:S(2)}) collective-permute-start(f32[4,16,128]{2,1,0:T(8,128)} %param.15), channel_id=1, source_target_pairs={{0,2},{1,3},{2,4},{3,5},{4,6},{5,7},{6,8},{7,9},{8,10},{9,11},{10,... | collective-permute-start | bytes 98312 | tf_op jit(solution)/shard_map/ppermute | solution.py:15
  112.9 18.8 %collective-permute-start.6 = (f32[4,16,128]{2,1,0:T(8,128)S(1)}, f32[4,16,128]{2,1,0:T(8,128)S(1)}, u32[]{:S(2)}, u32[]{:S(2)}) collective-permute-start(f32[4,16,128]{2,1,0:T(8,128)S(1)} %fusion.7), channel_id=1, source_target_pairs={{0,3},{1,4},{2,5},{3,6},{4,7},{5,8},{6,9},{7,10},{8,11},{9,12},{10... | collective-permute-start | bytes 98312 | tf_op jit(solution)/shard_map/ppermute | solution.py:15
  118.6 21.5 %collective-permute-start.11 = (f32[4,16,128]{2,1,0:T(8,128)S(1)}, f32[4,16,128]{2,1,0:T(8,128)S(1)}, u32[]{:S(2)}, u32[]{:S(2)}) collective-permute-start(f32[4,16,128]{2,1,0:T(8,128)S(1)} %fusion.7), channel_id=1, source_target_pairs={{3,0},{4,1},{5,2},{6,3},{7,4},{8,5},{9,6},{10,7},{11,8},{12,9},{13... | collective-permute-start | bytes 98312 | tf_op jit(solution)/shard_map/ppermute | solution.py:15
  122.3 17.7 %collective-permute-start.10 = (f32[4,16,128]{2,1,0:T(8,128)S(1)}, f32[4,16,128]{2,1,0:T(8,128)S(1)}, u32[]{:S(2)}, u32[]{:S(2)}) collective-permute-start(f32[4,16,128]{2,1,0:T(8,128)S(1)} %fusion.7), channel_id=1, source_target_pairs={{2,0},{3,1},{4,2},{5,3},{6,4},{7,5},{8,6},{9,7},{10,8},{11,9},{12,... | collective-permute-start | bytes 98312 | tf_op jit(solution)/shard_map/ppermute | solution.py:15
  126.2 13.9 %collective-permute-start.9 = (f32[4,16,128]{2,1,0:T(8,128)S(1)}, f32[4,16,128]{2,1,0:T(8,128)S(1)}, u32[]{:S(2)}, u32[]{:S(2)}) collective-permute-start(f32[4,16,128]{2,1,0:T(8,128)S(1)} %fusion.7), channel_id=1, source_target_pairs={{1,0},{2,1},{3,2},{4,3},{5,4},{6,5},{7,6},{8,7},{9,8},{10,9},{11,1... | collective-permute-start | bytes 98312 | tf_op jit(solution)/shard_map/ppermute | solution.py:15
  128.1 11.9 %collective-permute-start.8 = (f32[4,16,128]{2,1,0:T(8,128)S(1)}, f32[4,16,128]{2,1,0:T(8,128)S(1)}, u32[]{:S(2)}, u32[]{:S(2)}) collective-permute-start(f32[4,16,128]{2,1,0:T(8,128)S(1)} %fusion.7), channel_id=1, source_target_pairs={{0,1},{1,2},{2,3},{3,4},{4,5},{5,6},{6,7},{7,8},{8,9},{9,10},{10,1... | collective-permute-start | bytes 98312 | tf_op jit(solution)/shard_map/ppermute | solution.py:15
  191.3 19.9 %collective-permute-start.12 = (f32[4,16,128]{2,1,0:T(8,128)S(1)}, f32[4,16,128]{2,1,0:T(8,128)S(1)}, u32[]{:S(2)}, u32[]{:S(2)}) collective-permute-start(f32[4,16,128]{2,1,0:T(8,128)S(1)} %fusion.6), channel_id=1, source_target_pairs={{0,3},{1,4},{2,5},{3,6},{4,7},{5,8},{6,9},{7,10},{8,11},{9,12},{10... | collective-permute-start | bytes 98312 | tf_op jit(solution)/shard_map/ppermute | solution.py:15
  198.0 21.6 %collective-permute-start.17 = (f32[4,16,128]{2,1,0:T(8,128)S(1)}, f32[4,16,128]{2,1,0:T(8,128)S(1)}, u32[]{:S(2)}, u32[]{:S(2)}) collective-permute-start(f32[4,16,128]{2,1,0:T(8,128)S(1)} %fusion.6), channel_id=1, source_target_pairs={{3,0},{4,1},{5,2},{6,3},{7,4},{8,5},{9,6},{10,7},{11,8},{12,9},{13... | collective-permute-start | bytes 98312 | tf_op jit(solution)/shard_map/ppermute | solution.py:15
  201.2 18.4 %collective-permute-start.16 = (f32[4,16,128]{2,1,0:T(8,128)S(1)}, f32[4,16,128]{2,1,0:T(8,128)S(1)}, u32[]{:S(2)}, u32[]{:S(2)}) collective-permute-start(f32[4,16,128]{2,1,0:T(8,128)S(1)} %fusion.6), channel_id=1, source_target_pairs={{2,0},{3,1},{4,2},{5,3},{6,4},{7,5},{8,6},{9,7},{10,8},{11,9},{12,... | collective-permute-start | bytes 98312 | tf_op jit(solution)/shard_map/ppermute | solution.py:15
  205.6 13.9 %collective-permute-start.15 = (f32[4,16,128]{2,1,0:T(8,128)S(1)}, f32[4,16,128]{2,1,0:T(8,128)S(1)}, u32[]{:S(2)}, u32[]{:S(2)}) collective-permute-start(f32[4,16,128]{2,1,0:T(8,128)S(1)} %fusion.6), channel_id=1, source_target_pairs={{1,0},{2,1},{3,2},{4,3},{5,4},{6,5},{7,6},{8,7},{9,8},{10,9},{11,1... | collective-permute-start | bytes 98312 | tf_op jit(solution)/shard_map/ppermute | solution.py:15
  207.6 11.9 %collective-permute-start.14 = (f32[4,16,128]{2,1,0:T(8,128)S(1)}, f32[4,16,128]{2,1,0:T(8,128)S(1)}, u32[]{:S(2)}, u32[]{:S(2)}) collective-permute-start(f32[4,16,128]{2,1,0:T(8,128)S(1)} %fusion.6), channel_id=1, source_target_pairs={{0,1},{1,2},{2,3},{3,4},{4,5},{5,6},{6,7},{7,8},{8,9},{9,10},{10,1... | collective-permute-start | bytes 98312 | tf_op jit(solution)/shard_map/ppermute | solution.py:15
  230.3 10.1 %collective-permute-start.18 = (f32[4,16,128]{2,1,0:T(8,128)S(1)}, f32[4,16,128]{2,1,0:T(8,128)S(1)}, u32[]{:S(2)}, u32[]{:S(2)}) collective-permute-start(f32[4,16,128]{2,1,0:T(8,128)S(1)} %fusion.85), channel_id=1, source_target_pairs={{0,3},{1,4},{2,5},{3,6},{4,7},{8,11},{9,12},{10,13},{11,14},{12,15... | collective-permute-start | bytes 98312 | tf_op jit(solution)/shard_map/ppermute | solution.py:15
  231.7 13.7 %collective-permute-start.23 = (f32[4,16,128]{2,1,0:T(8,128)S(1)}, f32[4,16,128]{2,1,0:T(8,128)S(1)}, u32[]{:S(2)}, u32[]{:S(2)}) collective-permute-start(f32[4,16,128]{2,1,0:T(8,128)S(1)} %fusion.85), channel_id=1, source_target_pairs={{3,0},{4,1},{5,2},{6,3},{7,4},{11,8},{12,9},{13,10},{14,11},{15,12... | collective-permute-start | bytes 98312 | tf_op jit(solution)/shard_map/ppermute | solution.py:15
  233.0 12.4 %collective-permute-start.22 = (f32[4,16,128]{2,1,0:T(8,128)S(1)}, f32[4,16,128]{2,1,0:T(8,128)S(1)}, u32[]{:S(2)}, u32[]{:S(2)}) collective-permute-start(f32[4,16,128]{2,1,0:T(8,128)S(1)} %fusion.85), channel_id=1, source_target_pairs={{2,0},{3,1},{4,2},{5,3},{6,4},{7,5},{10,8},{11,9},{12,10},{13,11},... | collective-permute-start | bytes 98312 | tf_op jit(solution)/shard_map/ppermute | solution.py:15
  234.3 11.1 %collective-permute-start.21 = (f32[4,16,128]{2,1,0:T(8,128)S(1)}, f32[4,16,128]{2,1,0:T(8,128)S(1)}, u32[]{:S(2)}, u32[]{:S(2)}) collective-permute-start(f32[4,16,128]{2,1,0:T(8,128)S(1)} %fusion.85), channel_id=1, source_target_pairs={{1,0},{2,1},{3,2},{4,3},{5,4},{6,5},{7,6},{9,8},{10,9},{11,10},{12... | collective-permute-start | bytes 98312 | tf_op jit(solution)/shard_map/ppermute | solution.py:15
  236.3 9.1 %collective-permute-start.20 = (f32[4,16,128]{2,1,0:T(8,128)S(1)}, f32[4,16,128]{2,1,0:T(8,128)S(1)}, u32[]{:S(2)}, u32[]{:S(2)}) collective-permute-start(f32[4,16,128]{2,1,0:T(8,128)S(1)} %fusion.85), channel_id=1, source_target_pairs={{0,1},{1,2},{2,3},{3,4},{4,5},{5,6},{6,7},{8,9},{9,10},{10,11},{11... | collective-permute-start | bytes 98312 | tf_op jit(solution)/shard_map/ppermute | solution.py:15
  308.2 10.9 %collective-permute-start.24 = (f32[4,16,128]{2,1,0:T(8,128)S(1)}, f32[4,16,128]{2,1,0:T(8,128)S(1)}, u32[]{:S(2)}, u32[]{:S(2)}) collective-permute-start(f32[4,16,128]{2,1,0:T(8,128)S(1)} %fusion.3), channel_id=1, source_target_pairs={{0,3},{1,4},{2,5},{3,6},{4,7},{8,11},{9,12},{10,13},{11,14},{12,15... | collective-permute-start | bytes 98312 | tf_op jit(solution)/shard_map/ppermute | solution.py:15
  309.6 14.6 %collective-permute-start.29 = (f32[4,16,128]{2,1,0:T(8,128)S(1)}, f32[4,16,128]{2,1,0:T(8,128)S(1)}, u32[]{:S(2)}, u32[]{:S(2)}) collective-permute-start(f32[4,16,128]{2,1,0:T(8,128)S(1)} %fusion.3), channel_id=1, source_target_pairs={{3,0},{4,1},{5,2},{6,3},{7,4},{11,8},{12,9},{13,10},{14,11},{15,12... | collective-permute-start | bytes 98312 | tf_op jit(solution)/shard_map/ppermute | solution.py:15
  310.9 13.2 %collective-permute-start.28 = (f32[4,16,128]{2,1,0:T(8,128)S(1)}, f32[4,16,128]{2,1,0:T(8,128)S(1)}, u32[]{:S(2)}, u32[]{:S(2)}) collective-permute-start(f32[4,16,128]{2,1,0:T(8,128)S(1)} %fusion.3), channel_id=1, source_target_pairs={{2,0},{3,1},{4,2},{5,3},{6,4},{7,5},{10,8},{11,9},{12,10},{13,11},... | collective-permute-start | bytes 98312 | tf_op jit(solution)/shard_map/ppermute | solution.py:15
  312.2 11.9 %collective-permute-start.27 = (f32[4,16,128]{2,1,0:T(8,128)S(1)}, f32[4,16,128]{2,1,0:T(8,128)S(1)}, u32[]{:S(2)}, u32[]{:S(2)}) collective-permute-start(f32[4,16,128]{2,1,0:T(8,128)S(1)} %fusion.3), channel_id=1, source_target_pairs={{1,0},{2,1},{3,2},{4,3},{5,4},{6,5},{7,6},{9,8},{10,9},{11,10},{12... | collective-permute-start | bytes 98312 | tf_op jit(solution)/shard_map/ppermute | solution.py:15
  314.9 9.2 %collective-permute-start.26 = (f32[4,16,128]{2,1,0:T(8,128)S(1)}, f32[4,16,128]{2,1,0:T(8,128)S(1)}, u32[]{:S(2)}, u32[]{:S(2)}) collective-permute-start(f32[4,16,128]{2,1,0:T(8,128)S(1)} %fusion.3), channel_id=1, source_target_pairs={{0,1},{1,2},{2,3},{3,4},{4,5},{5,6},{6,7},{8,9},{9,10},{10,11},{11... | collective-permute-start | bytes 98312 | tf_op jit(solution)/shard_map/ppermute | solution.py:15
  353.3 18.6 %collective-permute-start.30 = (f32[4,16,128]{2,1,0:T(8,128)S(1)}, f32[4,16,128]{2,1,0:T(8,128)S(1)}, u32[]{:S(2)}, u32[]{:S(2)}) collective-permute-start(f32[4,16,128]{2,1,0:T(8,128)S(1)} %fusion.2), channel_id=1, source_target_pairs={{0,3},{1,4},{2,5},{3,6},{4,7},{5,8},{6,9},{7,10},{8,11},{9,12},{10... | collective-permute-start | bytes 98312 | tf_op jit(solution)/shard_map/ppermute | solution.py:15
  355.2 25.7 %collective-permute-start.35 = (f32[4,16,128]{2,1,0:T(8,128)S(1)}, f32[4,16,128]{2,1,0:T(8,128)S(1)}, u32[]{:S(2)}, u32[]{:S(2)}) collective-permute-start(f32[4,16,128]{2,1,0:T(8,128)S(1)} %fusion.2), channel_id=1, source_target_pairs={{3,0},{4,1},{5,2},{6,3},{7,4},{8,5},{9,6},{10,7},{11,8},{12,9},{13... | collective-permute-start | bytes 98312 | tf_op jit(solution)/shard_map/ppermute | solution.py:15
  362.4 18.4 %collective-permute-start.34 = (f32[4,16,128]{2,1,0:T(8,128)S(1)}, f32[4,16,128]{2,1,0:T(8,128)S(1)}, u32[]{:S(2)}, u32[]{:S(2)}) collective-permute-start(f32[4,16,128]{2,1,0:T(8,128)S(1)} %fusion.2), channel_id=1, source_target_pairs={{2,0},{3,1},{4,2},{5,3},{6,4},{7,5},{8,6},{9,7},{10,8},{11,9},{12,... | collective-permute-start | bytes 98312 | tf_op jit(solution)/shard_map/ppermute | solution.py:15
  364.4 16.4 %collective-permute-start.33 = (f32[4,16,128]{2,1,0:T(8,128)S(1)}, f32[4,16,128]{2,1,0:T(8,128)S(1)}, u32[]{:S(2)}, u32[]{:S(2)}) collective-permute-start(f32[4,16,128]{2,1,0:T(8,128)S(1)} %fusion.2), channel_id=1, source_target_pairs={{1,0},{2,1},{3,2},{4,3},{5,4},{6,5},{7,6},{8,7},{9,8},{10,9},{11,1... | collective-permute-start | bytes 98312 | tf_op jit(solution)/shard_map/ppermute | solution.py:15
  368.3 12.4 %collective-permute-start.32 = (f32[4,16,128]{2,1,0:T(8,128)S(1)}, f32[4,16,128]{2,1,0:T(8,128)S(1)}, u32[]{:S(2)}, u32[]{:S(2)}) collective-permute-start(f32[4,16,128]{2,1,0:T(8,128)S(1)} %fusion.2), channel_id=1, source_target_pairs={{0,1},{1,2},{2,3},{3,4},{4,5},{5,6},{6,7},{7,8},{8,9},{9,10},{10,1... | collective-permute-start | bytes 98312 | tf_op jit(solution)/shard_map/ppermute | solution.py:15
  371.9 8.9 %collective-permute-start.31 = (f32[4,16,128]{2,1,0:T(8,128)S(1)}, f32[4,16,128]{2,1,0:T(8,128)S(1)}, u32[]{:S(2)}, u32[]{:S(2)}) collective-permute-start(f32[4,16,128]{2,1,0:T(8,128)S(1)} %fusion.2), channel_id=1, source_target_pairs={{0,2},{1,3},{2,4},{3,5},{4,6},{5,7},{6,8},{7,9},{8,10},{9,11},{10,... | collective-permute-start | bytes 98312 | tf_op jit(solution)/shard_map/ppermute | solution.py:15
  (8 other events, 373.3 us)
